TPU v7x, 32 devices: a whole 2x2x4 slice. The times are simulated.
32 devices in a mesh: rep: 4 (over y, x), grp: 8 (over z, core).
Axes of the slice: x: 2, y: 2, z: 4, core: 2. Of those that a mesh axis runs over, the one named last changes fastest.
Arguments:
- block_in: bfloat16 [2, 4, 1024, 1024], P(None, 'rep', 'grp'), may hold values from -6 to 6
- cotangent: bfloat16 [2, 4, 1024, 1024], P(None, 'rep', 'grp'), may hold values from -6 to 6
- w_qkv: bfloat16 [2, 1024, 3072], P(None, 'grp'), may hold values from -0.1875 to 0.1875
- w_out: bfloat16 [2, 1024, 1024], P(None, 'grp'), may hold values from -0.1875 to 0.1875
- w_up: bfloat16 [2, 1024, 4096], P(None, 'grp'), may hold values from -0.1875 to 0.1875
- w_down: bfloat16 [2, 4096, 1024], P(None, 'grp'), may hold values from -0.09375 to 0.09375
- norm_gains: bfloat16 [2, 1024, 4], P(None, 'grp'), may hold values from 0.25 to 1.75
Outputs:
- block_out: bfloat16 [2, 4, 1024, 1024], P(None, 'rep', 'grp')
- block_in_grad: float32 [2, 4, 1024, 1024], P(None, 'rep', 'grp')
- w_qkv_grad: float32 [2, 1024, 3072], P(None, 'grp')
- w_out_grad: float32 [2, 1024, 1024], P(None, 'grp')
- w_up_grad: float32 [2, 1024, 4096], P(None, 'grp')
- w_down_grad: float32 [2, 4096, 1024], P(None, 'grp')
- norm_gains_grad: float32 [2, 1024, 4], P(None, 'grp')
All inputs are finite; a program needn't handle non-finite values.
Results may differ from a plain program's by a relative error of at most 0.023.
Values may be sent and summed in bfloat16 or wider, within the bound.
A program may use at most 384 MiB of HBM per device.

v0:
```python
import jax
import jax.numpy as jnp
from jax import lax
from jax.sharding import PartitionSpec as P

HEADS = 16
HDIM = 64
EPS = 1e-06
NEGATIVE = -1e30


def norm_apply(values, gains):
    return values * lax.rsqrt(jnp.mean(values * values, axis=-1, keepdims=True) + EPS) * gains


def inner_rows(left, right):
    return lax.dot_general(
        left, right, (((0,), (0,)), ((), ())), preferred_element_type=jnp.float32
    )


def times_trans(left, right):
    return lax.dot_general(
        left, right, (((1,), (1,)), ((), ())), preferred_element_type=jnp.float32
    )


def split_blocks(whole):
    length = whole.shape[0]
    width = min(512, length)
    count = length // width
    return (whole.reshape(count, width, HEADS, HDIM), width, count)


def block_at(blocks, index):
    return lax.dynamic_index_in_dim(blocks, index, 0, keepdims=False)


def key_scores(query, key_block, key_start, query_pos):
    scale = HDIM ** (-0.5)
    scores = (
        jnp.einsum("qhd,khd->hqk", query, key_block, preferred_element_type=jnp.float32) * scale
    )
    key_pos = key_start + jnp.arange(key_block.shape[0], dtype=jnp.int32)
    allowed = key_pos[None, :] <= query_pos[:, None]
    return (scores, allowed[None])


def attend(query, keys_all, values_all, query_pos):
    key_blocks, width, count = split_blocks(keys_all)
    value_blocks = split_blocks(values_all)[0]
    row_count = query.shape[0]
    upper = query_pos[row_count - 1] // width + 1

    def total_step(index, carry):
        running, total = carry
        scores, allowed = key_scores(query, block_at(key_blocks, index), index * width, query_pos)
        newest = jnp.maximum(running, jnp.max(jnp.where(allowed, scores, NEGATIVE), axis=-1))
        terms = jnp.where(allowed, jnp.exp(scores - newest[..., None]), 0.0)
        total = total * jnp.exp(running - newest) + jnp.sum(terms, axis=-1)
        return (newest, total)

    start_run = jnp.full((HEADS, row_count), NEGATIVE, jnp.float32)
    start_total = jnp.zeros((HEADS, row_count), jnp.float32)
    running, total = lax.fori_loop(0, upper, total_step, (start_run, start_total))
    log_total = running + jnp.log(total)

    def mix_step(index, accum):
        scores, allowed = key_scores(query, block_at(key_blocks, index), index * width, query_pos)
        probs = jnp.where(allowed, jnp.exp(scores - log_total[..., None]), 0.0)
        return accum + jnp.einsum(
            "hqk,khd->qhd",
            probs.astype(jnp.bfloat16),
            block_at(value_blocks, index),
            preferred_element_type=jnp.float32,
        )

    start_mix = jnp.zeros((row_count, HEADS, HDIM), jnp.float32)
    mixed = lax.fori_loop(0, upper, mix_step, start_mix)
    return (mixed.reshape(row_count, HEADS * HDIM), log_total)


def attend_back(query, keys_all, values_all, log_total, out_grad, delta, query_pos):
    key_blocks, width, count = split_blocks(keys_all)
    value_blocks = split_blocks(values_all)[0]
    row_count = query.shape[0]
    upper = query_pos[row_count - 1] // width + 1
    scale = HDIM ** (-0.5)

    def back_step(index, carry):
        query_acc, pieces = carry
        key_block = block_at(key_blocks, index)
        value_block = block_at(value_blocks, index)
        scores, allowed = key_scores(query, key_block, index * width, query_pos)
        probs = jnp.where(allowed, jnp.exp(scores - log_total[..., None]), 0.0)
        prob_grad = jnp.einsum(
            "qhd,khd->hqk", out_grad, value_block, preferred_element_type=jnp.float32
        )
        score_grad = (probs * (prob_grad - delta[..., None])).astype(jnp.bfloat16)
        query_acc = (
            query_acc
            + jnp.einsum("hqk,khd->qhd", score_grad, key_block, preferred_element_type=jnp.float32)
            * scale
        )
        key_grad = (
            jnp.einsum("hqk,qhd->khd", score_grad, query, preferred_element_type=jnp.float32)
            * scale
        )
        value_grad = jnp.einsum(
            "hqk,qhd->khd", probs.astype(jnp.bfloat16), out_grad, preferred_element_type=jnp.float32
        )
        joined = jnp.concatenate(
            [key_grad.reshape(width, HEADS * HDIM), value_grad.reshape(width, HEADS * HDIM)], axis=1
        )
        pieces = lax.dynamic_update_index_in_dim(pieces, joined, index, 0)
        return (query_acc, pieces)

    start_acc = jnp.zeros((row_count, HEADS, HDIM), jnp.float32)
    start_pieces = jnp.zeros((count, width, 2 * HEADS * HDIM), jnp.float32)
    query_grad, pieces = lax.fori_loop(0, upper, back_step, (start_acc, start_pieces))
    return (query_grad.reshape(row_count, HEADS * HDIM), pieces.reshape(-1, pieces.shape[-1]))


def layer_forward(hidden_in, weights, query_pos):
    w_qkv_full, w_out_full, w_up_full, w_down_full, gain_full = weights
    gains_f = gain_full.astype(jnp.float32)
    row_count = hidden_in.shape[0]
    width = w_out_full.shape[1]
    normed = norm_apply(hidden_in, gains_f[:, 0]).astype(jnp.bfloat16)
    qkv_low = jnp.dot(normed, w_qkv_full, preferred_element_type=jnp.float32).astype(jnp.bfloat16)
    query = qkv_low[:, :width]
    keys_all, values_all = (
        lax.all_gather(qkv_low[:, width : 2 * width], "grp", axis=0, tiled=True),
        lax.all_gather(qkv_low[:, 2 * width :], "grp", axis=0, tiled=True),
    )
    mixed, log_total = attend(
        query.reshape(row_count, HEADS, HDIM),
        keys_all.reshape(-1, HEADS, HDIM),
        values_all.reshape(-1, HEADS, HDIM),
        query_pos,
    )
    mixed_low = mixed.astype(jnp.bfloat16)
    attn_out = jnp.dot(mixed_low, w_out_full, preferred_element_type=jnp.float32)
    resid = hidden_in + norm_apply(attn_out, gains_f[:, 1])
    mlp_in = norm_apply(resid, gains_f[:, 2]).astype(jnp.bfloat16)
    up_out = jnp.dot(mlp_in, w_up_full, preferred_element_type=jnp.float32)
    active = jax.nn.gelu(up_out).astype(jnp.bfloat16)
    down_out = jnp.dot(active, w_down_full, preferred_element_type=jnp.float32)
    result = resid + norm_apply(down_out, gains_f[:, 3])
    kept = (
        hidden_in,
        normed,
        qkv_low,
        mixed,
        mixed_low,
        log_total,
        attn_out,
        resid,
        mlp_in,
        up_out,
        active,
        down_out,
    )
    return (result, kept)


def layer_backward(grad_out, weights, kept, query_pos):
    w_qkv_full, w_out_full, w_up_full, w_down_full, gain_full = weights
    (
        hidden_in,
        normed,
        qkv_low,
        mixed,
        mixed_low,
        log_total,
        attn_out,
        resid,
        mlp_in,
        up_out,
        active,
        down_out,
    ) = kept
    gains_f = gain_full.astype(jnp.float32)
    row_count = hidden_in.shape[0]
    width = w_out_full.shape[1]
    unused, puller = jax.vjp(norm_apply, down_out, gains_f[:, 3])
    down_grad, gain_four = puller(grad_out)
    down_low = down_grad.astype(jnp.bfloat16)
    w_down_grad = inner_rows(active, down_low)
    active_grad = times_trans(down_low, w_down_full)
    unused, puller = jax.vjp(jax.nn.gelu, up_out)
    up_low = puller(active_grad)[0].astype(jnp.bfloat16)
    w_up_grad = inner_rows(mlp_in, up_low)
    mlp_grad = times_trans(up_low, w_up_full)
    unused, puller = jax.vjp(norm_apply, resid, gains_f[:, 2])
    resid_part, gain_three = puller(mlp_grad)
    resid_grad = grad_out + resid_part
    unused, puller = jax.vjp(norm_apply, attn_out, gains_f[:, 1])
    attn_grad, gain_two = puller(resid_grad)
    attn_low = attn_grad.astype(jnp.bfloat16)
    w_out_grad = inner_rows(mixed_low, attn_low)
    mixed_grad = times_trans(attn_low, w_out_full).astype(jnp.bfloat16)
    keys_all, values_all = (
        lax.all_gather(qkv_low[:, width : 2 * width], "grp", axis=0, tiled=True),
        lax.all_gather(qkv_low[:, 2 * width :], "grp", axis=0, tiled=True),
    )
    delta = jnp.sum(
        (mixed_grad.astype(jnp.float32) * mixed).reshape(row_count, HEADS, HDIM), axis=-1
    ).T
    query_low = qkv_low[:, :width]
    query_grad, key_value_terms = attend_back(
        query_low.reshape(row_count, HEADS, HDIM),
        keys_all.reshape(-1, HEADS, HDIM),
        values_all.reshape(-1, HEADS, HDIM),
        log_total,
        mixed_grad.reshape(row_count, HEADS, HDIM),
        delta,
        query_pos,
    )
    key_value_grad = lax.psum_scatter(
        key_value_terms.astype(jnp.bfloat16), "grp", scatter_dimension=0, tiled=True
    ).astype(jnp.float32)
    qkv_grad = jnp.concatenate([query_grad, key_value_grad], axis=1).astype(jnp.bfloat16)
    w_qkv_grad = inner_rows(normed, qkv_grad)
    normed_grad = times_trans(qkv_grad, w_qkv_full)
    unused, puller = jax.vjp(norm_apply, hidden_in, gains_f[:, 0])
    input_part, gain_one = puller(normed_grad)
    gain_grad = jnp.stack([gain_one, gain_two, gain_three, gain_four], axis=1)
    return (resid_grad + input_part, (w_qkv_grad, w_out_grad, w_up_grad, w_down_grad, gain_grad))


def body(block_in, cotangent, w_qkv, w_out, w_up, w_down, norm_gains):
    layer_count = w_qkv.shape[0]
    micro_count = block_in.shape[0]
    row_count = block_in.shape[2]
    query_pos = lax.axis_index("grp") * row_count + jnp.arange(row_count, dtype=jnp.int32)
    totals = [None] * layer_count
    outputs = []
    input_grads = []
    for micro_idx in range(micro_count):
        hidden = block_in[micro_idx, 0].astype(jnp.float32)
        saved = []
        for layer_idx in range(layer_count):
            hidden, kept = layer_forward(
                hidden,
                (
                    lax.all_gather(w_qkv[layer_idx], "grp", axis=0, tiled=True),
                    lax.all_gather(w_out[layer_idx], "grp", axis=0, tiled=True),
                    lax.all_gather(w_up[layer_idx], "grp", axis=0, tiled=True),
                    lax.all_gather(w_down[layer_idx], "grp", axis=0, tiled=True),
                    lax.all_gather(norm_gains[layer_idx], "grp", axis=0, tiled=True),
                ),
                query_pos,
            )
            saved.append(kept)
        outputs.append(hidden.astype(jnp.bfloat16))
        grad_flow = cotangent[micro_idx, 0].astype(jnp.float32)
        for layer_idx in reversed(range(layer_count)):
            grad_flow, parts = layer_backward(
                grad_flow,
                (
                    lax.all_gather(w_qkv[layer_idx], "grp", axis=0, tiled=True),
                    lax.all_gather(w_out[layer_idx], "grp", axis=0, tiled=True),
                    lax.all_gather(w_up[layer_idx], "grp", axis=0, tiled=True),
                    lax.all_gather(w_down[layer_idx], "grp", axis=0, tiled=True),
                    lax.all_gather(norm_gains[layer_idx], "grp", axis=0, tiled=True),
                ),
                saved[layer_idx],
                query_pos,
            )
            if totals[layer_idx] is None:
                totals[layer_idx] = parts
            else:
                totals[layer_idx] = tuple(
                    (left + right for left, right in zip(totals[layer_idx], parts))
                )
        input_grads.append(grad_flow)
    reduced = []
    for layer_idx in range(layer_count):
        accum = totals[layer_idx]
        shards = (
            lax.psum_scatter(
                accum[0].astype(jnp.bfloat16), "grp", scatter_dimension=0, tiled=True
            ).astype(jnp.float32),
            lax.psum_scatter(
                accum[1].astype(jnp.bfloat16), "grp", scatter_dimension=0, tiled=True
            ).astype(jnp.float32),
            lax.psum_scatter(
                accum[2].astype(jnp.bfloat16), "grp", scatter_dimension=0, tiled=True
            ).astype(jnp.float32),
            lax.psum_scatter(
                accum[3].astype(jnp.bfloat16), "grp", scatter_dimension=0, tiled=True
            ).astype(jnp.float32),
            lax.psum_scatter(
                accum[4].astype(jnp.bfloat16), "grp", scatter_dimension=0, tiled=True
            ).astype(jnp.float32),
        )
        reduced.append(
            (
                lax.psum(shards[0].astype(jnp.bfloat16), "rep").astype(jnp.float32),
                lax.psum(shards[1].astype(jnp.bfloat16), "rep").astype(jnp.float32),
                lax.psum(shards[2].astype(jnp.bfloat16), "rep").astype(jnp.float32),
                lax.psum(shards[3].astype(jnp.bfloat16), "rep").astype(jnp.float32),
                lax.psum(shards[4].astype(jnp.bfloat16), "rep").astype(jnp.float32),
            )
        )
    block_out = jnp.stack(outputs)[:, None]
    block_in_grad = jnp.stack(input_grads)[:, None]
    stacked = [
        jnp.stack([reduced[layer_idx][member] for layer_idx in range(layer_count)])
        for member in range(5)
    ]
    return (block_out, block_in_grad, stacked[0], stacked[1], stacked[2], stacked[3], stacked[4])


def solution(mesh):
    return jax.shard_map(
        body,
        mesh=mesh,
        in_specs=(
            P(None, "rep", "grp", None),
            P(None, "rep", "grp", None),
            P(None, "grp", None),
            P(None, "grp", None),
            P(None, "grp", None),
            P(None, "grp", None),
            P(None, "grp", None),
        ),
        out_specs=(
            P(None, "rep", "grp", None),
            P(None, "rep", "grp", None),
            P(None, "grp", None),
            P(None, "grp", None),
            P(None, "grp", None),
            P(None, "grp", None),
            P(None, "grp", None),
        ),
        check_vma=False,
    )
```

profile of v0, /device:TPU:0, one launch (start us, length us, event | category | flops | bytes accessed | tf_op | source)
XLA Modules:
  0.0 1937.6 jit_solution(5514778637835726931)
XLA Ops:
  10.0 13.4 all-gather
  23.7 54.0 %all-gather.43.cloned.1.call-done = bf16[1,1024,3072]{2,1,0:T(8,128)(2,1)} async-done(((bf16[1,128,3072]{2,1,0:T(8,128)(2,1)}), bf16[1,1024,3072]{2,1,0:T(8,128)(2,1)}) %all-gather.43.cloned.1.call-update) | async-done | bytes 6291472 | tf_op jit(solution)/shard_map/all_gather | solution.py:247
  98.6 9.1 all-gather.5
  110.4 6.3 reshape.879
  123.4 17.8 all-gather.35.cloned.1.call-done
  156.6 15.3 all-gather.45.cloned.1.call-done
  174.8 27.8 %all-gather.29.cloned.1.call-done = bf16[1024,1024]{1,0:T(8,128)(2,1)} async-done(((bf16[128,1024]{1,0:T(8,128)(2,1)}), bf16[1024,1024]{1,0:T(8,128)(2,1)}) %all-gather.29.cloned.1.call-update) | async-done | bytes 2097168 | tf_op jit(solution)/shard_map/all_gather | solution.py:133
  214.5 18.2 all-gather.27.cloned.1.call-done
  255.1 60.7 %all-gather.47.cloned.1.call-done = bf16[1,1024,4096]{2,1,0:T(8,128)(2,1)} async-done(((bf16[1,128,4096]{2,1,0:T(8,128)(2,1)}), bf16[1,1024,4096]{2,1,0:T(8,128)(2,1)}) %all-gather.47.cloned.1.call-update) | async-done | bytes 8388624 | tf_op jit(solution)/shard_map/all_gather | solution.py:249
  320.6 78.0 %all-gather.49.cloned.1.call-done = bf16[1,4096,1024]{2,1,0:T(8,128)(2,1)} async-done(((bf16[1,512,1024]{2,1,0:T(8,128)(2,1)}), bf16[1,4096,1024]{2,1,0:T(8,128)(2,1)}) %all-gather.49.cloned.1.call-update) | async-done | bytes 8388624 | tf_op jit(solution)/shard_map/all_gather | solution.py:250
  413.7 49.9 %all-gather.51.cloned.1.call-done = bf16[1,1024,3072]{2,1,0:T(8,128)(2,1)} async-done(((bf16[1,128,3072]{2,1,0:T(8,128)(2,1)}), bf16[1,1024,3072]{2,1,0:T(8,128)(2,1)}) %all-gather.51.cloned.1.call-update) | async-done | bytes 6291472 | tf_op jit(solution)/shard_map/all_gather | solution.py:247
  477.1 19.1 all-gather.33.cloned.1.call-done
  509.4 17.1 all-gather.41.cloned.1.call-done
  526.5 6.3 reshape.881
  538.4 18.2 all-gather.39.cloned.1.call-done
  568.6 18.9 all-gather.31.cloned.1.call-done
  622.5 78.0 %all-gather.55.cloned.1.call-done = bf16[1,1024,4096]{2,1,0:T(8,128)(2,1)} async-done(((bf16[1,128,4096]{2,1,0:T(8,128)(2,1)}), bf16[1,1024,4096]{2,1,0:T(8,128)(2,1)}) %all-gather.55.cloned.1.call-update) | async-done | bytes 8388624 | tf_op jit(solution)/shard_map/all_gather | solution.py:249
  706.6 76.6 %all-gather.57.cloned.1.call-done = bf16[1,4096,1024]{2,1,0:T(8,128)(2,1)} async-done(((bf16[1,512,1024]{2,1,0:T(8,128)(2,1)}), bf16[1,4096,1024]{2,1,0:T(8,128)(2,1)}) %all-gather.57.cloned.1.call-update) | async-done | bytes 8388624 | tf_op jit(solution)/shard_map/all_gather | solution.py:250
  799.4 7.1 fusion.273
  806.5 7.5 fusion.287
  836.6 17.2 while.158
  857.3 18.7 while.156
  879.6 39.9 %reduce-scatter.23.cloned.1.call-done = bf16[128,2048]{1,0:T(8,128)(2,1)} async-done(((bf16[1024,2048]{1,0:T(8,128)(2,1)}), bf16[128,2048]{1,0:T(8,128)(2,1)}) %reduce-scatter.23.cloned.1.call-update) | async-done | bytes 524304 | tf_op jit(solution)/shard_map/reduce_scatter | solution.py:220
  925.6 44.9 %reduce-scatter.19.cloned.1.call-done = bf16[128,2048]{1,0:T(8,128)(2,1)} async-done(((bf16[1024,2048]{1,0:T(8,128)(2,1)}), bf16[128,2048]{1,0:T(8,128)(2,1)}) %reduce-scatter.19.cloned.1.call-update) | async-done | bytes 524304 | tf_op jit(solution)/shard_map/reduce_scatter | solution.py:220
  979.7 7.1 fusion.266
  1005.5 17.1 while.157
  1031.6 17.4 while.159
  1058.4 9.3 fusion.407
  1067.7 9.7 add_convert_fusion
  1078.5 9.5 fusion.405
  1088.0 11.5 add_convert_fusion.2
  1109.8 9.3 fusion.406
  1119.1 9.6 add_convert_fusion.1
  1129.7 9.5 fusion.404
  1139.3 11.5 add_convert_fusion.3
  1151.9 7.5 fusion.360
  1159.4 9.4 add_convert_fusion.5
  1181.9 30.3 %reduce-scatter.31.cloned.1.call-done = bf16[128,1024]{1,0:T(8,128)(2,1)} async-done(((bf16[1024,1024]{1,0:T(8,128)(2,1)}), bf16[128,1024]{1,0:T(8,128)(2,1)}) %reduce-scatter.31.cloned.1.call-update) | async-done | bytes 262160 | tf_op jit(solution)/shard_map/reduce_scatter | solution.py:285
  1212.2 90.7 %reduce-scatter.41.cloned.1.call-done = bf16[512,1024]{1,0:T(8,128)(2,1)} async-done(((bf16[4096,1024]{1,0:T(8,128)(2,1)}), bf16[512,1024]{1,0:T(8,128)(2,1)}) %reduce-scatter.41.cloned.1.call-update) | async-done | bytes 1048592 | tf_op jit(solution)/shard_map/reduce_scatter | solution.py:291
  1302.9 90.1 %reduce-scatter.37.cloned.1.call-done = bf16[128,4096]{1,0:T(8,128)(2,1)} async-done(((bf16[1024,4096]{1,0:T(8,128)(2,1)}), bf16[128,4096]{1,0:T(8,128)(2,1)}) %reduce-scatter.37.cloned.1.call-update) | async-done | bytes 1048592 | tf_op jit(solution)/shard_map/reduce_scatter | solution.py:288
  1393.0 70.5 %reduce-scatter.29.cloned.1.call-done = bf16[128,3072]{1,0:T(8,128)(2,1)} async-done(((bf16[1024,3072]{1,0:T(8,128)(2,1)}), bf16[128,3072]{1,0:T(8,128)(2,1)}) %reduce-scatter.29.cloned.1.call-update) | async-done | bytes 786448 | tf_op jit(solution)/shard_map/reduce_scatter | solution.py:282
  1463.5 90.2 %reduce-scatter.39.cloned.1.call-done = bf16[512,1024]{1,0:T(8,128)(2,1)} async-done(((bf16[4096,1024]{1,0:T(8,128)(2,1)}), bf16[512,1024]{1,0:T(8,128)(2,1)}) %reduce-scatter.39.cloned.1.call-update) | async-done | bytes 1048592 | tf_op jit(solution)/shard_map/reduce_scatter | solution.py:291
  1553.7 90.1 %reduce-scatter.35.cloned.1.call-done = bf16[128,4096]{1,0:T(8,128)(2,1)} async-done(((bf16[1024,4096]{1,0:T(8,128)(2,1)}), bf16[128,4096]{1,0:T(8,128)(2,1)}) %reduce-scatter.35.cloned.1.call-update) | async-done | bytes 1048592 | tf_op jit(solution)/shard_map/reduce_scatter | solution.py:288
  1643.8 70.5 %reduce-scatter.27.cloned.1.call-done = bf16[128,3072]{1,0:T(8,128)(2,1)} async-done(((bf16[1024,3072]{1,0:T(8,128)(2,1)}), bf16[128,3072]{1,0:T(8,128)(2,1)}) %reduce-scatter.27.cloned.1.call-update) | async-done | bytes 786448 | tf_op jit(solution)/shard_map/reduce_scatter | solution.py:282
  1716.2 29.7 %reduce-scatter.45.cloned.1.call-done = bf16[128,4]{1,0:T(8,128)(2,1)} async-done(((bf16[1024,4]{1,0:T(8,128)(2,1)}), bf16[128,4]{1,0:T(8,128)(2,1)}) %reduce-scatter.45.cloned.1.call-update) | async-done | bytes 1040
  1748.1 29.0 %reduce-scatter.43.cloned.1.call-done = bf16[128,4]{1,0:T(8,128)(2,1)} async-done(((bf16[1024,4]{1,0:T(8,128)(2,1)}), bf16[128,4]{1,0:T(8,128)(2,1)}) %reduce-scatter.43.cloned.1.call-update) | async-done | bytes 1040
  1777.9 9.9 all-reduce
  1788.4 132.3 %all-reduce.4.cloned.1.call-done = (bf16[1,128,3072]{2,1,0:T(8,128)(2,1)}, bf16[1,128,3072]{2,1,0:T(8,128)(2,1)}, bf16[1,128,1024]{2,1,0:T(8,128)(2,1)}, bf16[1,...) async-done(((bf16[1,128,3072]{2,1,0:T(8,128)(2,1)}, ...) | async-done | bytes 6291472 | tf_op jit(solution)/shard_map/psum | solution.py:300
  (801 shorter events, 416.1 us)
Async XLA Ops:
  7.2 70.5 %all-gather.43.cloned.1.call-start = ((), (), s32[]{:S(2)}) async-start(), calls=%async_computation.34 | async-start | bytes 7077888 | tf_op jit(solution)/shard_map/all_gather | solution.py:247
  9.9 100.5 %all-gather.37.cloned.1.call-start = ((), (), s32[]{:S(2)}) async-start(), calls=%async_computation.19 | async-start | bytes 2359296 | tf_op jit(solution)/shard_map/all_gather | solution.py:133
  23.7 230.2 %copy-start.148 = (f32[1024,1]{0,1:T(1,128)}, f32[1024,1]{0,1:T(1,128)S(1)}, u32[]{:S(2)}) copy-start(f32[1024,1]{0,1:T(1,128)S(1)} %get-tuple-element.1612) | copy-start | bytes 12292
  23.7 380.5 %copy-start.129 = (f32[1024,1]{0,1:T(1,128)}, f32[1024,1]{0,1:T(1,128)S(1)}, u32[]{:S(2)}) copy-start(f32[1024,1]{0,1:T(1,128)S(1)} %get-tuple-element.1610) | copy-start | bytes 12292
  23.7 389.6 %copy-start.150 = (f32[1024,1]{0,1:T(1,128)}, f32[1024,1]{0,1:T(1,128)S(1)}, u32[]{:S(2)}) copy-start(f32[1024,1]{0,1:T(1,128)S(1)} %get-tuple-element.1611) | copy-start | bytes 12292
  82.5 58.8 %all-gather.35.cloned.1.call-start = ((), (), s32[]{:S(2)}) async-start(), calls=%async_computation.18 | async-start | bytes 2359296 | tf_op jit(solution)/shard_map/all_gather | solution.py:134
  83.2 88.7 %all-gather.45.cloned.1.call-start = ((), (), s32[]{:S(2)}) async-start(), calls=%async_computation.35 | async-start | bytes 2359296 | tf_op jit(solution)/shard_map/all_gather | solution.py:248
  84.1 118.5 %all-gather.29.cloned.1.call-start = ((), (), s32[]{:S(2)}) async-start(), calls=%async_computation.15 | async-start | bytes 2359296 | tf_op jit(solution)/shard_map/all_gather | solution.py:133
  89.0 143.7 %all-gather.27.cloned.1.call-start = ((), (), s32[]{:S(2)}) async-start(), calls=%async_computation.14 | async-start | bytes 2359296 | tf_op jit(solution)/shard_map/all_gather | solution.py:134
  89.5 226.3 %all-gather.47.cloned.1.call-start = ((), (), s32[]{:S(2)}) async-start(), calls=%async_computation.36 | async-start | bytes 9437184 | tf_op jit(solution)/shard_map/all_gather | solution.py:249
  91.5 307.1 %all-gather.49.cloned.1.call-start = ((), (), s32[]{:S(2)}) async-start(), calls=%async_computation.37 | async-start | bytes 9437184 | tf_op jit(solution)/shard_map/all_gather | solution.py:250
  94.6 369.0 %all-gather.51.cloned.1.call-start = ((), (), s32[]{:S(2)}) async-start(), calls=%async_computation.38 | async-start | bytes 7077888 | tf_op jit(solution)/shard_map/all_gather | solution.py:247
  95.4 400.9 %all-gather.33.cloned.1.call-start = ((), (), s32[]{:S(2)}) async-start(), calls=%async_computation.17 | async-start | bytes 2359296 | tf_op jit(solution)/shard_map/all_gather | solution.py:133
  108.4 360.0 %copy-start.140 = (f32[1024,1]{0,1:T(1,128)}, f32[1024,1]{0,1:T(1,128)S(1)}, u32[]{:S(2)}) copy-start(f32[1024,1]{0,1:T(1,128)S(1)} %get-tuple-element.1609) | copy-start | bytes 12292
  255.1 149.1 %copy-start.205 = (f32[128]{0:T(128)}, f32[128]{0:T(128)S(1)}, u32[]{:S(2)}) copy-start(f32[128]{0:T(128)S(1)} %get-tuple-element.1557) | copy-start | bytes 1540
  255.1 158.2 %copy-start.32 = (f32[128,1024]{1,0:T(8,128)}, f32[128,1024]{1,0:T(8,128)S(1)}, u32[]{:S(2)}) copy-start(f32[128,1024]{1,0:T(8,128)S(1)} %get-tuple-element.1603) | copy-start | bytes 1572868
  320.6 83.1 %copy-start.72 = (f32[128,4096]{1,0:T(8,128)}, f32[128,4096]{1,0:T(8,128)S(1)}, u32[]{:S(2)}) copy-start(f32[128,4096]{1,0:T(8,128)S(1)} %fusion.228) | copy-start | bytes 6291460
  320.6 83.6 %copy-start.35 = (f32[128,1024]{1,0:T(8,128)S(1)}, f32[128,1024]{1,0:T(8,128)}, u32[]{:S(2)}) copy-start(f32[128,1024]{1,0:T(8,128)} %get-tuple-element.1558) | copy-start | bytes 1572868
  468.3 58.2 %all-gather.41.cloned.1.call-start = ((), (), s32[]{:S(2)}) async-start(), calls=%async_computation.21 | async-start | bytes 2359296 | tf_op jit(solution)/shard_map/all_gather | solution.py:133
  473.6 83.0 %all-gather.39.cloned.1.call-start = ((), (), s32[]{:S(2)}) async-start(), calls=%async_computation.20 | async-start | bytes 2359296 | tf_op jit(solution)/shard_map/all_gather | solution.py:134
  474.2 113.2 %all-gather.31.cloned.1.call-start = ((), (), s32[]{:S(2)}) async-start(), calls=%async_computation.16 | async-start | bytes 2359296 | tf_op jit(solution)/shard_map/all_gather | solution.py:134
  475.0 142.5 %all-gather.53.cloned.1.call-start = ((), (), s32[]{:S(2)}) async-start(), calls=%async_computation.39 | async-start | bytes 2359296 | tf_op jit(solution)/shard_map/all_gather | solution.py:248
  475.5 225.0 %all-gather.55.cloned.1.call-start = ((), (), s32[]{:S(2)}) async-start(), calls=%async_computation.40 | async-start | bytes 9437184 | tf_op jit(solution)/shard_map/all_gather | solution.py:249
  476.1 307.1 %all-gather.57.cloned.1.call-start = ((), (), s32[]{:S(2)}) async-start(), calls=%async_computation.41 | async-start | bytes 9437184 | tf_op jit(solution)/shard_map/all_gather | solution.py:250
  476.7 442.8 %reduce-scatter.23.cloned.1.call-start = ((), (), s32[]{:S(2)}) async-start(), calls=%async_computation.24 | async-start | bytes 4718592 | tf_op jit(solution)/shard_map/reduce_scatter | solution.py:220
  620.6 79.9 %copy-start.132 = (f32[1024,1]{0,1:T(1,128)S(1)}, f32[1024,1]{0,1:T(1,128)}, u32[]{:S(2)}) copy-start(f32[1024,1]{0,1:T(1,128)} %get-tuple-element.1607) | copy-start | bytes 12292
  622.5 198.1 %copy-start.38 = (f32[128,1024]{1,0:T(8,128)}, f32[128,1024]{1,0:T(8,128)S(1)}, u32[]{:S(2)}) copy-start(f32[128,1024]{1,0:T(8,128)S(1)} %get-tuple-element.1633) | copy-start | bytes 1572868
  622.5 198.1 %copy-start.176 = (f32[128]{0:T(128)}, f32[128]{0:T(128)S(1)}, u32[]{:S(2)}) copy-start(f32[128]{0:T(128)S(1)} %fusion.394) | copy-start | bytes 1540
  853.9 116.5 %reduce-scatter.19.cloned.1.call-start = ((), (), s32[]{:S(2)}) async-start(), calls=%async_computation.22 | async-start | bytes 4718592 | tf_op jit(solution)/shard_map/reduce_scatter | solution.py:220
  876.1 275.2 %reduce-scatter.21.cloned.1.call-start = ((), (), s32[]{:S(2)}) async-start(), calls=%async_computation.23 | async-start | bytes 4718592 | tf_op jit(solution)/shard_map/reduce_scatter | solution.py:220
  879.3 91.1 %copy-start.111 = (bf16[128,1024]{1,0:T(8,128)(2,1)}, bf16[128,1024]{1,0:T(8,128)(2,1)S(1)}, u32[]{:S(2)}) copy-start(bf16[128,1024]{1,0:T(8,128)(2,1)S(1)} %copy.250) | copy-start | bytes 786436
  879.5 90.9 %copy-start.44 = (f32[128,1024]{1,0:T(8,128)S(1)}, f32[128,1024]{1,0:T(8,128)}, u32[]{:S(2)}) copy-start(f32[128,1024]{1,0:T(8,128)} %copy-done.42) | copy-start | bytes 1572868
  879.5 90.9 %copy-start.48 = (f32[128,1024]{1,0:T(8,128)S(1)}, f32[128,1024]{1,0:T(8,128)}, u32[]{:S(2)}) copy-start(f32[128,1024]{1,0:T(8,128)} %copy-done.46) | copy-start | bytes 1572868
  879.5 90.9 %copy-start.141 = (f32[1024,1]{0,1:T(1,128)S(1)}, f32[1024,1]{0,1:T(1,128)}, u32[]{:S(2)}) copy-start(f32[1024,1]{0,1:T(1,128)} %copy-done.140) | copy-start | bytes 12292
  879.6 90.9 %copy-start.179 = (f32[128]{0:T(128)S(1)}, f32[128]{0:T(128)}, u32[]{:S(2)}) copy-start(f32[128]{0:T(128)} %copy-done.178) | copy-start | bytes 1540
  879.6 90.9 %copy-start.184 = (f32[128]{0:T(128)S(1)}, f32[128]{0:T(128)}, u32[]{:S(2)}) copy-start(f32[128]{0:T(128)} %copy-done.183) | copy-start | bytes 1540
  1022.6 136.8 %reduce-scatter.25.cloned.1.call-start = ((), (), s32[]{:S(2)}) async-start(), calls=%async_computation.25 | async-start | bytes 4718592 | tf_op jit(solution)/shard_map/reduce_scatter | solution.py:220
  1049.1 132.8 %reduce-scatter.33.cloned.1.call-start = ((), (), s32[]{:S(2)}) async-start(), calls=%async_computation.29 | async-start | bytes 2359296 | tf_op jit(solution)/shard_map/reduce_scatter | solution.py:285
  1052.9 159.3 %reduce-scatter.31.cloned.1.call-start = ((), (), s32[]{:S(2)}) async-start(), calls=%async_computation.28 | async-start | bytes 2359296 | tf_op jit(solution)/shard_map/reduce_scatter | solution.py:285
  1056.8 246.1 %reduce-scatter.41.cloned.1.call-start = ((), (), s32[]{:S(2)}) async-start(), calls=%async_computation.33 | async-start | bytes 9437184 | tf_op jit(solution)/shard_map/reduce_scatter | solution.py:291
  1077.5 315.6 %reduce-scatter.37.cloned.1.call-start = ((), (), s32[]{:S(2)}) async-start(), calls=%async_computation.31 | async-start | bytes 9437184 | tf_op jit(solution)/shard_map/reduce_scatter | solution.py:288
  1099.5 364.0 %reduce-scatter.29.cloned.1.call-start = ((), (), s32[]{:S(2)}) async-start(), calls=%async_computation.27 | async-start | bytes 7077888 | tf_op jit(solution)/shard_map/reduce_scatter | solution.py:282
  1108.2 445.5 %reduce-scatter.39.cloned.1.call-start = ((), (), s32[]{:S(2)}) async-start(), calls=%async_computation.32 | async-start | bytes 9437184 | tf_op jit(solution)/shard_map/reduce_scatter | solution.py:291
  1128.7 515.1 %reduce-scatter.35.cloned.1.call-start = ((), (), s32[]{:S(2)}) async-start(), calls=%async_computation.30 | async-start | bytes 9437184 | tf_op jit(solution)/shard_map/reduce_scatter | solution.py:288
  1150.8 563.5 %reduce-scatter.27.cloned.1.call-start = ((), (), s32[]{:S(2)}) async-start(), calls=%async_computation.26 | async-start | bytes 7077888 | tf_op jit(solution)/shard_map/reduce_scatter | solution.py:282
  1168.9 577.0 %reduce-scatter.45.cloned.1.call-start = ((), (), s32[]{:S(2)}) async-start(), calls=%async_computation.43 | async-start | bytes 294912
  1170.5 606.6 %reduce-scatter.43.cloned.1.call-start = ((), (), s32[]{:S(2)}) async-start(), calls=%async_computation.42 | async-start | bytes 294912
  1181.8 738.9 %all-reduce.4.cloned.1.call-start = ((), (), s32[]{:S(2)}) async-start(), calls=%async_computation.44 | async-start | bytes 12582912 | tf_op jit(solution)/shard_map/psum | solution.py:300
  (212 other events, 2450.5 us)
Sparse Core Ops, SparseCore 0:
  10.2 67.4 all-gather.42
  82.6 27.8 all-gather.36
  112.6 28.5 all-gather.34
  143.3 28.5 all-gather.44
  174.0 28.5 all-gather.28
  204.0 28.5 all-gather.26
  234.3 81.5 all-gather.46
  318.0 80.5 all-gather.48
  400.3 63.2 all-gather.50
  468.4 27.7 all-gather.32
  497.8 28.6 all-gather.40
  528.0 28.5 all-gather.38
  558.8 28.6 all-gather.30
  588.9 28.5 all-gather.52
  618.9 81.5 all-gather.54
  702.6 80.5 all-gather.56
  854.0 65.4 reduce-scatter.22
  922.2 48.1 reduce-scatter.18
  1022.7 64.9 reduce-scatter.20
  1090.4 48.1 reduce-scatter.24
  1141.5 33.9 reduce-scatter.32
  1177.7 34.4 reduce-scatter.30
  1214.5 88.3 reduce-scatter.40
  1305.0 87.9 reduce-scatter.36
  1395.3 68.1 reduce-scatter.28
  1465.7 87.9 reduce-scatter.38
  1555.8 87.9 reduce-scatter.34
  1646.1 68.1 reduce-scatter.26
  1717.1 28.6 reduce-scatter.44
  1748.6 28.4 reduce-scatter.42
  1781.5 139.1 all-reduce.3
where the time goes:
time: 1950 us; the launch traced here: 1940 us
  waiting for transfers between devices  1370 us (70%)
  matrix products  293 us (15%)
  local copies, waits for them, and re-layouts  187 us (10%)
  blocking collectives  32.5 us (2%)
  other arithmetic  28.8 us (1%)
  between operations  20.1 us (1%)
    reduce_scatter x2, waiting for transfers between devices, body(): lax.psum_scatter(accum[3].astype(jnp.bfloat16), 'grp', scatter_dimension=...  181 us
    reduce_scatter x2, waiting for transfers between devices, body(): lax.psum_scatter(accum[2].astype(jnp.bfloat16), 'grp', scatter_dimension=...  180 us
    all_gather x2, waiting for transfers between devices, body(): lax.all_gather(w_down[layer_idx], 'grp', axis=0, tiled=True)  155 us
    reduce_scatter x2, waiting for transfers between devices, body(): lax.psum_scatter(accum[0].astype(jnp.bfloat16), 'grp', scatter_dimension=...  141 us
    all_gather x2, waiting for transfers between devices, body(): lax.all_gather(w_up[layer_idx], 'grp', axis=0, tiled=True)  139 us
    psum x1, waiting for transfers between devices, body(): lax.psum(shards[0].astype(jnp.bfloat16), 'rep').astype(jnp.float32)  132 us
    dot_general x16, matrix products, inner_rows(): lax.dot_general(left, right, (((0,), (0,)), ((), ())), preferred_element_...  110 us
    all_gather x2, waiting for transfers between devices, body(): lax.all_gather(w_qkv[layer_idx], 'grp', axis=0, tiled=True)  104 us
  transfers between devices with their start and end apart: 31, of which 28 were waited for; matrix products, arithmetic and copies ran while one was open for 18% of the time, Pallas kernels for 0%

commit v1 on v0

--- a/solution.py
+++ b/solution.py
@@ -1,3 +1,4 @@
+import functools
 import jax
 import jax.numpy as jnp
 from jax import lax
@@ -7,6 +8,28 @@
 HDIM = 64
 EPS = 1e-06
 NEGATIVE = -1e30
+
+
+def recover_group(w_in, axis_id):
+    buffer = []
+    lanes = jax.lax.axis_size(axis_id)
+    for no in range(lanes):
+        buffer.append((no, (no + 1) % lanes))
+    table = []
+    for no in range(lanes):
+        table.append((no, (no - 1) % lanes))
+    s_next, formed = ([w_in], [w_in])
+    for _ in range(lanes // 2):
+        z = jax.lax.ppermute(s_next[-1], axis_id, perm=buffer)
+        s_next.append(z)
+    for _ in range((lanes - 1) // 2):
+        formed.append(jax.lax.ppermute(formed[-1], axis_id, perm=table))
+    mid_arr = jnp.concatenate([*s_next[::-1], *formed[1:]], 0)
+    main = jnp.roll(mid_arr, (jax.lax.axis_index(axis_id) - lanes // 2) * w_in.shape[0], 0)
+    return main
+
+
+supply_circles = functools.partial(recover_group, axis_id="grp")
 
 
 def norm_apply(values, gains):
@@ -130,7 +153,7 @@
     qkv_low = jnp.dot(normed, w_qkv_full, preferred_element_type=jnp.float32).astype(jnp.bfloat16)
     query = qkv_low[:, :width]
     keys_all, values_all = (
-        lax.all_gather(qkv_low[:, width : 2 * width], "grp", axis=0, tiled=True),
+        supply_circles(qkv_low[:, width : 2 * width]),
         lax.all_gather(qkv_low[:, 2 * width :], "grp", axis=0, tiled=True),
     )
     mixed, log_total = attend(

time: 1950 us -> 1970 us (1.010)
  waiting for transfers between devices: 1370 us -> 1270 us
  local copies, waits for them, and re-layouts: 187 us -> 252 us
    ppermute x0 -> x28, waiting for transfers between devices: none -> 162 us  [the longest x16 150 us: recover_group(): z = jax.lax.ppermute(s_next[-1], axis_id, perm=buffer)]
    all_gather x2, waiting for transfers between devices: 139 us -> 61.4 us  [body(): lax.all_gather(w_up[layer_idx], 'grp', axis=0, tiled=True)]
    all_gather x4, waiting for transfers between devices: 73.1 us -> 0.06 us  [layer_forward(): lax.all_gather(qkv_low[:, 2 * width:], 'grp', axis=0, tiled=True)]
    all_gather x4, waiting for transfers between devices: 65.7 us -> 0.06 us  [layer_backward(): lax.all_gather(qkv_low[:, width:2 * width], 'grp', axis=0, tiled=True)]
    unnamed x434 -> x458, local copies, waits for them, and re-layouts: 69.6 us -> 104 us
    reduce_scatter x4, waiting for transfers between devices: 84.8 us -> 60.1 us  [layer_backward(): lax.psum_scatter(key_value_terms.astype(jnp.bfloat16), 'grp', scatter_dim...]
    another operation x8 -> x12, local copies, waits for them, and re-layouts: 50.8 us -> 71.9 us  [split_blocks(): return (whole.reshape(count, width, HEADS, HDIM), width, count)]
    all_gather x2, waiting for transfers between devices: 21 us -> 0.01 us  [body(): lax.all_gather(w_out[layer_idx], 'grp', axis=0, tiled=True)]
  transfers between devices with their start and end apart: 31 -> 59, of which waited for: 28 -> 38; matrix products, arithmetic and copies ran while one was open for 18% -> 25% of each run, Pallas kernels for 0% -> 0%
where the time goes in v1:
time: 1970 us; the launch traced here: 1960 us
  waiting for transfers between devices  1270 us (64%)
  matrix products  305 us (15%)
  local copies, waits for them, and re-layouts  252 us (13%)
  blocking collectives  47 us (2%)
  other arithmetic  44.1 us (2%)
  between operations  20.6 us (1%)
  starting transfers between devices  19.9 us (1%)
    reduce_scatter x2, waiting for transfers between devices, body(): lax.psum_scatter(accum[3].astype(jnp.bfloat16), 'grp', scatter_dimension=...  181 us
    reduce_scatter x2, waiting for transfers between devices, body(): lax.psum_scatter(accum[2].astype(jnp.bfloat16), 'grp', scatter_dimension=...  180 us
    all_gather x2, waiting for transfers between devices, body(): lax.all_gather(w_down[layer_idx], 'grp', axis=0, tiled=True)  153 us
    ppermute x16, waiting for transfers between devices, recover_group(): z = jax.lax.ppermute(s_next[-1], axis_id, perm=buffer)  150 us
    reduce_scatter x2, waiting for transfers between devices, body(): lax.psum_scatter(accum[0].astype(jnp.bfloat16), 'grp', scatter_dimension=...  141 us
    psum x1, waiting for transfers between devices, body(): lax.psum(shards[0].astype(jnp.bfloat16), 'rep').astype(jnp.float32)  132 us
    dot_general x16, matrix products, inner_rows(): lax.dot_general(left, right, (((0,), (0,)), ((), ())), preferred_element_...  110 us
    unnamed x458, local copies, waits for them, and re-layouts  104 us
  transfers between devices with their start and end apart: 59, of which 38 were waited for; matrix products, arithmetic and copies ran while one was open for 25% of the time, Pallas kernels for 0%

profile of v1, /device:TPU:0, one launch (start us, length us, event | category | flops | bytes accessed | tf_op | source)
XLA Modules:
  0.0 1957.1 jit_solution(6013018066608556295)
XLA Ops:
  10.0 13.4 all-gather
  24.2 53.5 %all-gather.43.cloned.1.call-done = bf16[1,1024,3072]{2,1,0:T(8,128)(2,1)} async-done(((bf16[1,128,3072]{2,1,0:T(8,128)(2,1)}), bf16[1,1024,3072]{2,1,0:T(8,128)(2,1)}) %all-gather.43.cloned.1.call-update) | async-done | bytes 6291472 | tf_op jit(solution)/shard_map/all_gather | solution.py:270
  89.3 7.6 collective-permute-done.15
  96.9 7.6 collective-permute-done.16
  104.5 7.6 collective-permute-done.17
  119.9 10.2 collective-permute-done
  130.1 13.2 collective-permute-done.1
  143.3 7.6 collective-permute-done.2
  150.9 7.6 collective-permute-done.3
  167.4 23.6 %all-gather.5 = bf16[1,1024,4]{1,2,0:T(4,128)(2,1)S(1)} all-gather(bf16[1,128,4]{1,2,0:T(4,128)(2,1)S(1)} %get-tuple-element.1637), channel_id=7, replica_groups=mesh['rep'=4,'grp'=8] {'grp'}, dimensions={1}, use_global_device_ids=true | all-gather | bytes 9216 | tf_op jit(solution)/shard_map/all_gather | solution.py:274
  282.9 27.3 %all-gather.47.cloned.1.call-done = bf16[1,1024,4096]{2,1,0:T(8,128)(2,1)} async-done(((bf16[1,128,4096]{2,1,0:T(8,128)(2,1)}), bf16[1,1024,4096]{2,1,0:T(8,128)(2,1)}) %all-gather.47.cloned.1.call-update) | async-done | bytes 8388624 | tf_op jit(solution)/shard_map/all_gather | solution.py:272
  316.3 76.5 %all-gather.49.cloned.1.call-done = bf16[1,4096,1024]{2,1,0:T(8,128)(2,1)} async-done(((bf16[1,512,1024]{2,1,0:T(8,128)(2,1)}), bf16[1,4096,1024]{2,1,0:T(8,128)(2,1)}) %all-gather.49.cloned.1.call-update) | async-done | bytes 8388624 | tf_op jit(solution)/shard_map/all_gather | solution.py:273
  408.6 49.2 %all-gather.51.cloned.1.call-done = bf16[1,1024,3072]{2,1,0:T(8,128)(2,1)} async-done(((bf16[1,128,3072]{2,1,0:T(8,128)(2,1)}), bf16[1,1024,3072]{2,1,0:T(8,128)(2,1)}) %all-gather.51.cloned.1.call-update) | async-done | bytes 6291472 | tf_op jit(solution)/shard_map/all_gather | solution.py:270
  467.5 11.1 collective-permute-done.21
  478.5 13.2 collective-permute-done.22
  499.4 7.7 collective-permute-done.24
  511.6 13.2 collective-permute-done.7
  532.4 7.6 collective-permute-done.9
  540.0 13.2 collective-permute-done.10
  680.1 34.1 %all-gather.55.cloned.1.call-done = bf16[1,1024,4096]{2,1,0:T(8,128)(2,1)} async-done(((bf16[1,128,4096]{2,1,0:T(8,128)(2,1)}), bf16[1,1024,4096]{2,1,0:T(8,128)(2,1)}) %all-gather.55.cloned.1.call-update) | async-done | bytes 8388624 | tf_op jit(solution)/shard_map/all_gather | solution.py:272
  720.3 76.5 %all-gather.57.cloned.1.call-done = bf16[1,4096,1024]{2,1,0:T(8,128)(2,1)} async-done(((bf16[1,512,1024]{2,1,0:T(8,128)(2,1)}), bf16[1,4096,1024]{2,1,0:T(8,128)(2,1)}) %all-gather.57.cloned.1.call-update) | async-done | bytes 8388624 | tf_op jit(solution)/shard_map/all_gather | solution.py:273
  820.4 7.8 fusion.287
  845.7 17.4 while.158
  870.6 18.8 while.156
  918.1 15.1 reduce-scatter.23.cloned.1.call-done
  939.2 44.9 %reduce-scatter.19.cloned.1.call-done = bf16[128,2048]{1,0:T(8,128)(2,1)} async-done(((bf16[1024,2048]{1,0:T(8,128)(2,1)}), bf16[128,2048]{1,0:T(8,128)(2,1)}) %reduce-scatter.19.cloned.1.call-update) | async-done | bytes 524304 | tf_op jit(solution)/shard_map/reduce_scatter | solution.py:243
  1024.8 17.1 while.157
  1051.0 17.6 while.159
  1078.0 9.3 fusion.411
  1087.4 9.7 add_convert_fusion
  1098.2 9.5 fusion.409
  1107.7 11.5 add_convert_fusion.2
  1129.6 9.3 fusion.410
  1138.9 9.6 add_convert_fusion.1
  1149.6 9.5 fusion.408
  1159.1 11.6 add_convert_fusion.3
  1179.3 9.4 add_convert_fusion.5
  1201.9 30.0 %reduce-scatter.31.cloned.1.call-done = bf16[128,1024]{1,0:T(8,128)(2,1)} async-done(((bf16[1024,1024]{1,0:T(8,128)(2,1)}), bf16[128,1024]{1,0:T(8,128)(2,1)}) %reduce-scatter.31.cloned.1.call-update) | async-done | bytes 262160 | tf_op jit(solution)/shard_map/reduce_scatter | solution.py:308
  1231.9 90.5 %reduce-scatter.41.cloned.1.call-done = bf16[512,1024]{1,0:T(8,128)(2,1)} async-done(((bf16[4096,1024]{1,0:T(8,128)(2,1)}), bf16[512,1024]{1,0:T(8,128)(2,1)}) %reduce-scatter.41.cloned.1.call-update) | async-done | bytes 1048592 | tf_op jit(solution)/shard_map/reduce_scatter | solution.py:314
  1322.3 90.1 %reduce-scatter.37.cloned.1.call-done = bf16[128,4096]{1,0:T(8,128)(2,1)} async-done(((bf16[1024,4096]{1,0:T(8,128)(2,1)}), bf16[128,4096]{1,0:T(8,128)(2,1)}) %reduce-scatter.37.cloned.1.call-update) | async-done | bytes 1048592 | tf_op jit(solution)/shard_map/reduce_scatter | solution.py:311
  1412.4 70.5 %reduce-scatter.29.cloned.1.call-done = bf16[128,3072]{1,0:T(8,128)(2,1)} async-done(((bf16[1024,3072]{1,0:T(8,128)(2,1)}), bf16[128,3072]{1,0:T(8,128)(2,1)}) %reduce-scatter.29.cloned.1.call-update) | async-done | bytes 786448 | tf_op jit(solution)/shard_map/reduce_scatter | solution.py:305
  1483.0 90.1 %reduce-scatter.39.cloned.1.call-done = bf16[512,1024]{1,0:T(8,128)(2,1)} async-done(((bf16[4096,1024]{1,0:T(8,128)(2,1)}), bf16[512,1024]{1,0:T(8,128)(2,1)}) %reduce-scatter.39.cloned.1.call-update) | async-done | bytes 1048592 | tf_op jit(solution)/shard_map/reduce_scatter | solution.py:314
  1573.1 90.1 %reduce-scatter.35.cloned.1.call-done = bf16[128,4096]{1,0:T(8,128)(2,1)} async-done(((bf16[1024,4096]{1,0:T(8,128)(2,1)}), bf16[128,4096]{1,0:T(8,128)(2,1)}) %reduce-scatter.35.cloned.1.call-update) | async-done | bytes 1048592 | tf_op jit(solution)/shard_map/reduce_scatter | solution.py:311
  1663.2 70.5 %reduce-scatter.27.cloned.1.call-done = bf16[128,3072]{1,0:T(8,128)(2,1)} async-done(((bf16[1024,3072]{1,0:T(8,128)(2,1)}), bf16[128,3072]{1,0:T(8,128)(2,1)}) %reduce-scatter.27.cloned.1.call-update) | async-done | bytes 786448 | tf_op jit(solution)/shard_map/reduce_scatter | solution.py:305
  1735.6 29.7 %reduce-scatter.45.cloned.1.call-done = bf16[128,4]{1,0:T(8,128)(2,1)} async-done(((bf16[1024,4]{1,0:T(8,128)(2,1)}), bf16[128,4]{1,0:T(8,128)(2,1)}) %reduce-scatter.45.cloned.1.call-update) | async-done | bytes 1040
  1767.5 29.0 %reduce-scatter.43.cloned.1.call-done = bf16[128,4]{1,0:T(8,128)(2,1)} async-done(((bf16[1024,4]{1,0:T(8,128)(2,1)}), bf16[128,4]{1,0:T(8,128)(2,1)}) %reduce-scatter.43.cloned.1.call-update) | async-done | bytes 1040
  1797.4 9.9 all-reduce
  1807.9 132.3 %all-reduce.4.cloned.1.call-done = (bf16[1,128,3072]{2,1,0:T(8,128)(2,1)}, bf16[1,128,3072]{2,1,0:T(8,128)(2,1)}, bf16[1,128,1024]{2,1,0:T(8,128)(2,1)}, bf16[1,...) async-done(((bf16[1,128,3072]{2,1,0:T(8,128)(2,1)}, ...) | async-done | bytes 6291472 | tf_op jit(solution)/shard_map/psum | solution.py:323
  (902 shorter events, 587.6 us)
Async XLA Ops:
  7.2 70.5 %all-gather.43.cloned.1.call-start = ((), (), s32[]{:S(2)}) async-start(), calls=%async_computation.34 | async-start | bytes 7077888 | tf_op jit(solution)/shard_map/all_gather | solution.py:270
  9.9 233.2 %all-gather.31.cloned.1.call-start = ((), (), s32[]{:S(2)}) async-start(), calls=%async_computation.16 | async-start | bytes 2359296 | tf_op jit(solution)/shard_map/all_gather | solution.py:157
  81.6 7.6 collective-permute-start.14
  115.9 139.1 %all-gather.27.cloned.1.call-start = ((), (), s32[]{:S(2)}) async-start(), calls=%async_computation.14 | async-start | bytes 2359296 | tf_op jit(solution)/shard_map/all_gather | solution.py:157
  119.9 10.2 collective-permute-start
  130.1 13.2 collective-permute-start.1
  160.8 110.6 %all-gather.45.cloned.1.call-start = ((), (), s32[]{:S(2)}) async-start(), calls=%async_computation.35 | async-start | bytes 2359296 | tf_op jit(solution)/shard_map/all_gather | solution.py:271
  161.7 148.5 %all-gather.47.cloned.1.call-start = ((), (), s32[]{:S(2)}) async-start(), calls=%async_computation.36 | async-start | bytes 9437184 | tf_op jit(solution)/shard_map/all_gather | solution.py:272
  165.0 227.8 %all-gather.49.cloned.1.call-start = ((), (), s32[]{:S(2)}) async-start(), calls=%async_computation.37 | async-start | bytes 9437184 | tf_op jit(solution)/shard_map/all_gather | solution.py:273
  166.6 291.2 %all-gather.51.cloned.1.call-start = ((), (), s32[]{:S(2)}) async-start(), calls=%async_computation.38 | async-start | bytes 7077888 | tf_op jit(solution)/shard_map/all_gather | solution.py:270
  166.7 24.4 %collective-permute-start.18 = (bf16[128,1024]{1,0:T(8,128)(2,1)S(1)}, bf16[128,1024]{1,0:T(8,128)(2,1)S(1)}, u32[]{:S(2)}, u32[]{:S(2)}) collective-permute-start(bf16[128,1024]{1,0:T(8,128)(2,1)S(1)} %slice.228), channel_id=1, source_target_pairs={{0,7},{1,0},{2,1},{3,2},{4,3},{5,4},{6,5},{7,6},{8,15},{9,8},{10,9... | collective-permute-start | bytes 786440 | tf_op jit(solution)/shard_map/ppermute | solution.py:26
  166.7 24.3 %collective-permute-start.4 = (bf16[128,1024]{1,0:T(8,128)(2,1)S(1)}, bf16[128,1024]{1,0:T(8,128)(2,1)S(1)}, u32[]{:S(2)}, u32[]{:S(2)}) collective-permute-start(bf16[128,1024]{1,0:T(8,128)(2,1)S(1)} %slice.107), channel_id=1, source_target_pairs={{0,7},{1,0},{2,1},{3,2},{4,3},{5,4},{6,5},{7,6},{8,15},{9,8},{10,9... | collective-permute-start | bytes 786440 | tf_op jit(solution)/shard_map/ppermute | solution.py:26
  167.4 451.6 %all-gather.35.cloned.1.call-start = ((), (), s32[]{:S(2)}) async-start(), calls=%async_computation.18 | async-start | bytes 2359296 | tf_op jit(solution)/shard_map/all_gather | solution.py:227
  191.1 11.0 collective-permute-start.5
  194.9 8.7 collective-permute-start.20
  202.1 19.0 collective-permute-start.6
  462.4 168.7 %all-gather.39.cloned.1.call-start = ((), (), s32[]{:S(2)}) async-start(), calls=%async_computation.22 | async-start | bytes 2359296 | tf_op jit(solution)/shard_map/all_gather | solution.py:227
  467.1 175.0 %all-gather.33.cloned.1.call-start = ((), (), s32[]{:S(2)}) async-start(), calls=%async_computation.17 | async-start | bytes 2359296 | tf_op jit(solution)/shard_map/all_gather | solution.py:157
  467.2 11.4 collective-permute-start.21
  478.5 13.2 collective-permute-start.22
  499.4 7.7 collective-permute-start.24
  510.8 147.4 %all-gather.53.cloned.1.call-start = ((), (), s32[]{:S(2)}) async-start(), calls=%async_computation.39 | async-start | bytes 2359296 | tf_op jit(solution)/shard_map/all_gather | solution.py:271
  511.5 149.7 %all-gather.29.cloned.1.call-start = ((), (), s32[]{:S(2)}) async-start(), calls=%async_computation.15 | async-start | bytes 2359296 | tf_op jit(solution)/shard_map/all_gather | solution.py:157
  511.6 13.2 collective-permute-start.7
  540.0 13.2 collective-permute-start.10
  555.4 158.7 %all-gather.55.cloned.1.call-start = ((), (), s32[]{:S(2)}) async-start(), calls=%async_computation.40 | async-start | bytes 9437184 | tf_op jit(solution)/shard_map/all_gather | solution.py:272
  556.2 240.6 %all-gather.57.cloned.1.call-start = ((), (), s32[]{:S(2)}) async-start(), calls=%async_computation.41 | async-start | bytes 9437184 | tf_op jit(solution)/shard_map/all_gather | solution.py:273
  556.8 332.8 %all-gather.37.cloned.1.call-start = ((), (), s32[]{:S(2)}) async-start(), calls=%async_computation.20 | async-start | bytes 2359296 | tf_op jit(solution)/shard_map/all_gather | solution.py:227
  557.3 343.1 %all-gather.41.cloned.1.call-start = ((), (), s32[]{:S(2)}) async-start(), calls=%async_computation.24 | async-start | bytes 2359296 | tf_op jit(solution)/shard_map/all_gather | solution.py:227
  557.5 8.3 collective-permute-start.11
  565.8 7.7 collective-permute-start.12
  569.6 12.2 collective-permute-start.27
  573.4 359.8 %reduce-scatter.23.cloned.1.call-start = ((), (), s32[]{:S(2)}) async-start(), calls=%async_computation.23 | async-start | bytes 4718592 | tf_op jit(solution)/shard_map/reduce_scatter | solution.py:243
  573.4 25.8 %collective-permute-start.13 = (bf16[128,1024]{1,0:T(8,128)(2,1)}, bf16[128,1024]{1,0:T(8,128)(2,1)}, u32[]{:S(2)}, u32[]{:S(2)}) collective-permute-start(bf16[128,1024]{1,0:T(8,128)(2,1)} %collective-permute-done.12), channel_id=1, source_target_pairs={{0,7},{1,0},{2,1},{3,2},{4,3},{5,4},{6,5},{7,6},{8,15},{9,8},{10,9... | collective-permute-start | bytes 786440 | tf_op jit(solution)/shard_map/ppermute | solution.py:26
  867.2 116.9 %reduce-scatter.19.cloned.1.call-start = ((), (), s32[]{:S(2)}) async-start(), calls=%async_computation.19 | async-start | bytes 4718592 | tf_op jit(solution)/shard_map/reduce_scatter | solution.py:243
  889.4 282.0 %reduce-scatter.21.cloned.1.call-start = ((), (), s32[]{:S(2)}) async-start(), calls=%async_computation.21 | async-start | bytes 4718592 | tf_op jit(solution)/shard_map/reduce_scatter | solution.py:243
  1042.0 137.3 %reduce-scatter.25.cloned.1.call-start = ((), (), s32[]{:S(2)}) async-start(), calls=%async_computation.25 | async-start | bytes 4718592 | tf_op jit(solution)/shard_map/reduce_scatter | solution.py:243
  1068.7 133.1 %reduce-scatter.33.cloned.1.call-start = ((), (), s32[]{:S(2)}) async-start(), calls=%async_computation.29 | async-start | bytes 2359296 | tf_op jit(solution)/shard_map/reduce_scatter | solution.py:308
  1072.6 159.3 %reduce-scatter.31.cloned.1.call-start = ((), (), s32[]{:S(2)}) async-start(), calls=%async_computation.28 | async-start | bytes 2359296 | tf_op jit(solution)/shard_map/reduce_scatter | solution.py:308
  1076.5 245.9 %reduce-scatter.41.cloned.1.call-start = ((), (), s32[]{:S(2)}) async-start(), calls=%async_computation.33 | async-start | bytes 9437184 | tf_op jit(solution)/shard_map/reduce_scatter | solution.py:314
  1097.2 315.3 %reduce-scatter.37.cloned.1.call-start = ((), (), s32[]{:S(2)}) async-start(), calls=%async_computation.31 | async-start | bytes 9437184 | tf_op jit(solution)/shard_map/reduce_scatter | solution.py:311
  1119.3 363.7 %reduce-scatter.29.cloned.1.call-start = ((), (), s32[]{:S(2)}) async-start(), calls=%async_computation.27 | async-start | bytes 7077888 | tf_op jit(solution)/shard_map/reduce_scatter | solution.py:305
  1128.0 445.1 %reduce-scatter.39.cloned.1.call-start = ((), (), s32[]{:S(2)}) async-start(), calls=%async_computation.32 | async-start | bytes 9437184 | tf_op jit(solution)/shard_map/reduce_scatter | solution.py:314
  1148.6 514.6 %reduce-scatter.35.cloned.1.call-start = ((), (), s32[]{:S(2)}) async-start(), calls=%async_computation.30 | async-start | bytes 9437184 | tf_op jit(solution)/shard_map/reduce_scatter | solution.py:311
  1170.7 563.0 %reduce-scatter.27.cloned.1.call-start = ((), (), s32[]{:S(2)}) async-start(), calls=%async_computation.26 | async-start | bytes 7077888 | tf_op jit(solution)/shard_map/reduce_scatter | solution.py:305
  1188.8 576.4 %reduce-scatter.45.cloned.1.call-start = ((), (), s32[]{:S(2)}) async-start(), calls=%async_computation.43 | async-start | bytes 294912
  1190.4 606.1 %reduce-scatter.43.cloned.1.call-start = ((), (), s32[]{:S(2)}) async-start(), calls=%async_computation.42 | async-start | bytes 294912
  1201.8 738.4 %all-reduce.4.cloned.1.call-start = ((), (), s32[]{:S(2)}) async-start(), calls=%async_computation.44 | async-start | bytes 12582912 | tf_op jit(solution)/shard_map/psum | solution.py:323
  (241 other events, 4515.4 us)
Sparse Core Ops, SparseCore 0:
  10.2 67.4 all-gather.42
  116.0 32.7 all-gather.30
  160.9 29.6 all-gather.26
  192.6 32.6 all-gather.44
  226.8 83.3 all-gather.46
  312.2 80.5 all-gather.48
  394.5 63.2 all-gather.50
  462.6 33.6 all-gather.34
  497.9 30.2 all-gather.38
  529.7 34.4 all-gather.32
  565.8 31.9 all-gather.52
  599.2 31.7 all-gather.28
  632.6 81.5 all-gather.54
  716.2 80.5 all-gather.56
  798.3 27.6 all-gather.36
  827.4 28.6 all-gather.40
  867.3 65.8 reduce-scatter.22
  935.9 48.1 reduce-scatter.18
  1042.2 64.9 reduce-scatter.20
  1109.9 48.1 reduce-scatter.24
  1160.9 33.9 reduce-scatter.32
  1197.2 34.6 reduce-scatter.30
  1234.2 88.1 reduce-scatter.40
  1324.5 87.9 reduce-scatter.36
  1414.7 68.1 reduce-scatter.28
  1485.1 87.9 reduce-scatter.38
  1575.2 87.9 reduce-scatter.34
  1665.5 68.1 reduce-scatter.26
  1736.5 28.6 reduce-scatter.44
  1768.0 28.4 reduce-scatter.42
  1801.0 139.1 all-reduce.3
